TPU v7x, 32 devices: a whole 2x2x4 slice. The times are simulated.
32 devices in a mesh: seq: 8 (over y, x, core), tp: 4 (over z).
Axes of the slice: x: 2, y: 2, z: 4, core: 2. Of those that a mesh axis runs over, the one named last changes fastest.
Arguments:
- grad_out: bfloat16 [1024, 8192], P('seq', 'tp'), may hold values from -6 to 6
- resid_in: bfloat16 [1024, 8192], P('seq', 'tp'), may hold values from -6 to 6
- down_weight: bfloat16 [28672, 8192], P('seq', 'tp'), may hold values from -0.03125 to 0.03125
- hidden_clean: bfloat16 [28672, 512], P('seq', 'tp'), may hold values from -6 to 6
- hidden_corrupt: bfloat16 [28672, 512], P('seq', 'tp'), may hold values from -6 to 6
- patched: int32 [14336], replicated, may hold values from 0 to 28671, as said below
Outputs:
- resid_scores: float32 [1024], P('seq')
- token_scores: float32 [512], P('tp')
- neuron_scores: float32 [28672], P('seq')
Inputs may be any that keep to these rules, and one draw needn't show every extreme that they name: `patched`: 14336 distinct hidden-unit indices.
All inputs are finite; a program needn't handle non-finite values.
Results may differ from a plain program's by a relative error of at most 0.0046.
Values may be sent and summed in bfloat16 or wider, within the bound.
A program may use at most 128 MiB of HBM per device.

v0:
```python
import functools
import math

import jax
import jax.numpy as jnp
from jax import lax
from jax.experimental import pallas as pl
from jax.experimental.pallas import tpu as pltpu
from jax.sharding import PartitionSpec as P

F32 = jnp.float32
BF16 = jnp.bfloat16
NT = (((1,), (1,)), ((), ()))


def each(count, body):
    def step(index, carry):
        body(index)
        return carry

    lax.fori_loop(0, count, step, 0)


def kernel(
    S, T, C, G, L, R, scales,
    grad_hbm, resid_hbm, weight_hbm, clean_hbm, corrupt_hbm, patched_hbm,
    resid_out, token_out, neuron_out,
    grad, resid, weight, clean, corrupt, patched,
    partner_grad, partner_resid, means, diff, unit, mask, acc, token, token_in, token_sum,
    total_in, message, message_in, counts,
    load_sem, weight_sem, pair_send, pair_recv, mean_send, mean_recv, diff_send, diff_recv,
    msg_send, msg_recv, tok_send, tok_recv, sum_send, sum_recv,
):
    seq = lax.axis_index("seq")
    tp = lax.axis_index("tp")
    pairs = S // 2
    partner = lax.rem(seq + pairs, S)
    upper = seq // pairs
    rows = grad.shape[0]
    half = rows // 2
    units = weight.shape[0]
    piece = units // C
    local_len = diff.shape[2]

    def local(source, target, index):
        return pltpu.make_async_copy(source, target, load_sem.at[index])

    loads = [
        local(clean_hbm, clean, 0),
        local(corrupt_hbm, corrupt, 1),
        local(grad_hbm, grad, 2),
        local(resid_hbm, resid, 3),
        local(patched_hbm, patched, 4),
    ]
    for load in loads:
        load.start()

    def piece_rows(c):
        return pl.ds(pl.multiple_of(c * piece, 16), piece)

    def weight_load(c):
        return pltpu.make_async_copy(
            weight_hbm.at[piece_rows(c)], weight.at[piece_rows(c)], weight_sem.at[c]
        )

    def remote(source, target, send, recv, device):
        return pltpu.make_async_remote_copy(
            src_ref=source, dst_ref=target, send_sem=send, recv_sem=recv,
            device_id=device, device_id_type=pl.DeviceIdType.MESH,
        )

    barrier = pltpu.get_barrier_semaphore()

    def greet_seq(i):
        pl.semaphore_signal(
            barrier, inc=1, device_id=(lax.rem(seq + i + 1, S), tp),
            device_id_type=pl.DeviceIdType.MESH,
        )

    def greet_tp(i):
        pl.semaphore_signal(
            barrier, inc=1, device_id=(seq, lax.rem(tp + i + 1, T)),
            device_id_type=pl.DeviceIdType.MESH,
        )

    each(S - 1, greet_seq)
    each(T - 1, greet_tp)
    loads[0].wait()
    loads[1].wait()

    def subtract(c):
        r = piece_rows(c)
        diff[tp, r, :] = (clean[r, :].astype(F32) - corrupt[r, :].astype(F32)).astype(BF16)

    each(C, subtract)
    loads[2].wait()
    loads[3].wait()
    pl.semaphore_wait(barrier, S - 1 + T - 1)

    send_start = pl.multiple_of((1 - upper) * half, 8)
    keep_start = pl.multiple_of(upper * half, 8)
    grad_copy = remote(
        grad.at[pl.ds(send_start, half)], partner_grad, pair_send.at[0], pair_recv.at[0],
        (partner, tp),
    )
    resid_copy = remote(resid, partner_resid, pair_send.at[1], pair_recv.at[1], (partner, tp))
    grad_copy.start()

    def diff_copy(block, c, step):
        place = diff.at[block, piece_rows(c)]
        direction = (step + 1) // 2
        return remote(
            place, place, diff_send.at[direction, block, c], diff_recv.at[block, c],
            (seq, tp + step),
        )

    def forward(block, c, step):
        @pl.when((tp + step >= 0) & (tp + step < T))
        def _():
            diff_copy(block, c, step).start()

    def own(c):
        forward(tp, c, 1)
        forward(tp, c, -1)

    each(C, own)

    def relay(s, c):
        @pl.when(tp - s >= 0)
        def _():
            diff_copy(tp - s, c, 1).wait_recv()
            forward(tp - s, c, 1)

        @pl.when(tp + s < T)
        def _():
            diff_copy(tp + s, c, -1).wait_recv()
            forward(tp + s, c, -1)

    each(C, lambda c: weight_load(c).start())

    grad_copy.wait()
    slot = lax.rem(seq, pairs) * 2 + upper
    kept = grad[pl.ds(keep_start, half), :].astype(F32)
    means[slot] = ((kept + partner_grad[...].astype(F32)) * 0.5).astype(BF16)

    def mean_copy(i):
        return remote(
            means.at[slot], means.at[slot], mean_send.at[i], mean_recv.at[slot],
            (lax.rem(seq + i, S), tp),
        )

    each(S - 1, lambda i: mean_copy(i + 1).start())
    resid_copy.start()

    loads[4].wait()
    counts[...] = jnp.zeros_like(counts)
    width = patched.shape[1]
    group_ids = lax.broadcasted_iota(jnp.int32, (G, width), 0)
    lane_ids = lax.broadcasted_iota(jnp.int32, (L, width), 0)

    def count(k):
        ids = patched[pl.ds(k, 1), :] - seq * units + S * units
        high = ids // L - (S * units) // L
        low = lax.rem(ids, L)
        counts[...] += lax.dot_general(
            jnp.where(high == group_ids, 1.0, 0.0).astype(BF16),
            jnp.where(low == lane_ids, 1.0, 0.0).astype(BF16),
            NT, preferred_element_type=F32,
        )

    each(patched.shape[0], count)

    def spread(g):
        row = jnp.broadcast_to(counts[pl.ds(g, 1), :], (128, L))
        mask[pl.ds(pl.multiple_of(g * L, 8), L), :] = row.T

    each(G, spread)
    acc[...] = jnp.zeros_like(acc)
    token[...] = jnp.zeros_like(token)

    each(C, lambda c: relay(1, c))

    def await_mean(i):
        source = lax.rem(seq + i + 1, S)
        place = means.at[lax.rem(source, pairs) * 2 + source // pairs]
        sem = mean_recv.at[lax.rem(source, pairs) * 2 + source // pairs]
        remote(place, place, mean_send.at[0], sem, (source, tp)).wait_recv()

    each(S - 1, await_mean)

    def multiply(c):
        weight_load(c).wait()
        r = piece_rows(c)
        left = weight[r, :]
        block_slots = 2 * pairs // T
        for b in range(T):
            right = means[b * block_slots : (b + 1) * block_slots]
            right = right.reshape(local_len, right.shape[-1])
            unit[b, r, :] = lax.dot_general(left, right, NT, preferred_element_type=F32)
        relay(2, c)

    each(C, multiply)

    def product(block, c):
        r = piece_rows(c)
        value = diff[block, r, :].astype(F32) * unit[block, r, :]
        masks = mask[r, :]
        for k in range(local_len // 128):
            part = value[:, k * 128 : (k + 1) * 128]
            acc[r, :] += part
            token[block, :, k * 128 : (k + 1) * 128] += jnp.sum(
                part * masks, axis=0, keepdims=True
            )

    def products(s, c):
        if s == 0:
            product(tp, c)
            return

        @pl.when(tp - s >= 0)
        def _():
            product(tp - s, c)

        @pl.when(tp + s < T)
        def _():
            product(tp + s, c)

    resid_copy.wait()
    sign = (1 - 2 * upper).astype(F32)

    def resid_rows(k):
        r = pl.ds(pl.multiple_of(k * L, 8), L)
        difference = resid[r, :].astype(F32) - partner_resid[r, :].astype(F32)
        terms = sign * difference * grad[r, :].astype(F32)
        folded = terms[:, 0:128]
        for j in range(1, terms.shape[1] // 128):
            folded = folded + terms[:, j * 128 : (j + 1) * 128]
        message[pl.ds(G + k, 1), :] = jnp.sum(folded.T, axis=0, keepdims=True)

    each(R, resid_rows)
    for s in range(min(3, T)):
        each(C, lambda c: products(s, c))
    for s in range(3, T):

        def last(c):
            relay(s, c)
            products(s, c)

        each(C, last)

    def fold(g):
        block = acc[pl.ds(pl.multiple_of(g * L, 8), L), :]
        message[pl.ds(g, 1), :] = jnp.sum(block.T, axis=0, keepdims=True)

    def token_copy(i):
        target = lax.rem(tp + i, T)
        return remote(
            token.at[target], token_in.at[tp], tok_send.at[i], tok_recv.at[tp], (seq, target)
        )

    each(T - 1, lambda i: token_copy(i + 1).start())
    each(G, fold)

    def message_copy(i):
        return remote(
            message, message_in.at[tp], msg_send.at[i], msg_recv.at[tp],
            (seq, lax.rem(tp + i, T)),
        )

    each(T - 1, lambda i: message_copy(i + 1).start())

    token_in[tp] = token[tp]

    def await_token(i):
        source = lax.rem(tp + i + 1, T)
        remote(
            token.at[0], token_in.at[source], tok_send.at[0], tok_recv.at[source], (seq, source)
        ).wait_recv()

    each(T - 1, await_token)
    token_sum[...] = jnp.sum(token_in[...], axis=0)

    def sum_copy(i):
        return remote(
            token_sum, total_in.at[seq], sum_send.at[i], sum_recv.at[seq],
            (lax.rem(seq + i, S), tp),
        )

    each(S - 1, lambda i: sum_copy(i + 1).start())
    total_in[seq] = token_sum[...]
    message_in[tp] = message[...]

    def await_message(i):
        source = lax.rem(tp + i + 1, T)
        remote(
            message, message_in.at[source], msg_send.at[0], msg_recv.at[source], (seq, source)
        ).wait_recv()

    each(T - 1, await_message)
    total = jnp.sum(message_in[...], axis=0)
    neuron_out[...] = total[:G] * scales[2]
    resid_out[...] = total[G:] * scales[0]

    def await_sum(i):
        source = lax.rem(seq + i + 1, S)
        remote(
            token_sum, total_in.at[source], sum_send.at[0], sum_recv.at[source], (source, tp)
        ).wait_recv()

    each(S - 1, await_sum)
    token_out[...] = jnp.sum(total_in[...], axis=0) * scales[1]

    each(S - 1, lambda i: mean_copy(i + 1).wait_send())
    each(T - 1, lambda i: token_copy(i + 1).wait_send())
    each(T - 1, lambda i: message_copy(i + 1).wait_send())
    each(S - 1, lambda i: sum_copy(i + 1).wait_send())

    def drain(c):
        def sent(block, step):
            @pl.when((tp + step >= 0) & (tp + step < T) & (block >= 0) & (block < T))
            def _():
                diff_copy(block, c, step).wait_send()

        for s in range(T):
            sent(tp - s, 1)
            sent(tp + s, -1)

    each(C, drain)


def shards(grad_out, resid_in, down_weight, hidden_clean, hidden_corrupt, patched):
    S = lax.axis_size("seq")
    T = lax.axis_size("tp")
    rows, width = grad_out.shape
    units, local_len = hidden_clean.shape
    C = max(c for c in range(1, 9) if units % (16 * c) == 0)
    L = math.gcd(units, 128)
    G = units // L
    R = rows // L
    lanes = math.gcd(patched.shape[0], 1024)
    half = rows // 2
    scales = (
        1.0 / math.sqrt(width * T),
        1.0 / math.sqrt(patched.shape[0]),
        1.0 / math.sqrt(local_len * T),
    )
    dma = lambda *shape: pltpu.SemaphoreType.DMA(shape)
    resid, token, neuron = pl.pallas_call(
        functools.partial(kernel, S, T, C, G, L, R, scales),
        out_shape=(
            jax.ShapeDtypeStruct((R, L), F32),
            jax.ShapeDtypeStruct((1, local_len), F32),
            jax.ShapeDtypeStruct((G, L), F32),
        ),
        in_specs=[pl.BlockSpec(memory_space=pl.ANY)] * 6,
        out_specs=[pl.BlockSpec(memory_space=pltpu.VMEM)] * 3,
        scratch_shapes=[
            pltpu.VMEM((rows, width), BF16),
            pltpu.VMEM((rows, width), BF16),
            pltpu.VMEM((units, width), BF16),
            pltpu.VMEM((units, local_len), BF16),
            pltpu.VMEM((units, local_len), BF16),
            pltpu.VMEM((patched.shape[0] // lanes, lanes), jnp.int32),
            pltpu.VMEM((half, width), BF16),
            pltpu.VMEM((rows, width), BF16),
            pltpu.VMEM((S, half, width), BF16),
            pltpu.VMEM((T, units, local_len), BF16),
            pltpu.VMEM((T, units, local_len), F32),
            pltpu.VMEM((units, 128), F32),
            pltpu.VMEM((units, 128), F32),
            pltpu.VMEM((T, 1, local_len), F32),
            pltpu.VMEM((T, 1, local_len), F32),
            pltpu.VMEM((1, local_len), F32),
            pltpu.VMEM((S, 1, local_len), F32),
            pltpu.VMEM((G + R, L), F32),
            pltpu.VMEM((T, G + R, L), F32),
            pltpu.VMEM((G, L), F32),
            dma(5), dma(C), dma(2), dma(2), dma(S), dma(S), dma(2, T, C), dma(T, C),
            dma(T), dma(T), dma(T), dma(T), dma(S), dma(S),
        ],
        compiler_params=pltpu.CompilerParams(
            collective_id=0, has_side_effects=True, vmem_limit_bytes=56 * 1024 * 1024
        ),
    )(
        grad_out, resid_in, down_weight, hidden_clean, hidden_corrupt,
        patched.reshape(-1, lanes),
    )
    return (resid.reshape(rows), token.reshape(local_len), neuron.reshape(units))


def solution(mesh):
    in_specs = (P("seq", "tp"), P("seq", "tp"), P("seq", "tp"), P("seq", "tp"), P("seq", "tp"), P())
    out_specs = (P("seq"), P("tp"), P("seq"))
    return jax.shard_map(shards, mesh=mesh, in_specs=in_specs, out_specs=out_specs, check_vma=False)
```

profile of v0, /device:TPU:0, one launch (start us, length us, event | category | flops | bytes accessed | tf_op | source)
XLA Modules:
  0.0 81.5 jit_solution(15676757433085297908)
XLA Ops:
  0.6 1.4 %reshape.18.patched_hbm = s32[14,1024]{1,0:T(8,128)} reshape(s32[14336]{0:T(1024)} %param.11) | data formatting | bytes 114688 | tf_op jit(solution)/shard_map/reshape | solution.py:386
  2.1 75.8 %shard_map.85 = (f32[1,128]{1,0:T(1,128)}, f32[1,128]{1,0:T(1,128)}, f32[28,128]{1,0:T(8,128)}) custom-call(bf16[128,2048]{1,0:T(8,128)(2,1)} %grad_hbm.1, bf16[128,2048]{1,0:T(8,128)(2,1)} %resid_hbm.1, bf16[3584,2048]{1,0:T(8,128)(2,1)} %weight_hbm.1, bf16[3584,128]{1,0:T(8,128)(2,1)} %clean_hbm.1, bf16[3584,128]{1,0:T(8,128)(2,1)} %corrupt_hbm.1, ...), custom_call_target="tpu_custom_call" | custom-call | tf_op jit(solution)/shard_map/pallas_call | solution.py:348
  77.9 1.1 %copy.12 = f32[128]{0:T(128)} copy(f32[128]{0:T(128)} %bitcast.5) | data formatting | bytes 1024
  79.0 1.2 %copy.13 = f32[128]{0:T(128)} copy(f32[128]{0:T(128)} %bitcast.4) | data formatting | bytes 1024
  80.2 1.3 %copy.14 = f32[3584]{0:T(1024)} copy(f32[3584]{0:T(1024)} %bitcast.3) | data formatting | bytes 28672
where the time goes:
time: 81.8 us; the launch traced here: 81.5 us
  Pallas kernels  75.8 us (93%)
  local copies, waits for them, and re-layouts  5.07 us (6%)
    pallas_call x1, Pallas kernels, shards(): pl.pallas_call(functools.partial(kernel, S, T, C, G, L, R, scales), out_s...  75.8 us
    unnamed x3, local copies, waits for them, and re-layouts  3.62 us

commit v1 on v0

--- a/solution.py
+++ b/solution.py
@@ -22,14 +22,14 @@
 
 
 def kernel(
-    S, T, C, G, L, R, scales,
+    S, T, C, G, L, scales,
     grad_hbm, resid_hbm, weight_hbm, clean_hbm, corrupt_hbm, patched_hbm,
     resid_out, token_out, neuron_out,
     grad, resid, weight, clean, corrupt, patched,
-    partner_grad, partner_resid, means, diff, unit, mask, acc, token, token_in, token_sum,
-    total_in, message, message_in, counts,
-    load_sem, weight_sem, pair_send, pair_recv, mean_send, mean_recv, diff_send, diff_recv,
-    msg_send, msg_recv, tok_send, tok_recv, sum_send, sum_recv,
+    partner_grad, partner_resid, means, diff, unit, partial, partial_in, mask, acc, token, token_in, token_sum,
+    total_in, message, message_in, counts, scored, score_out,
+    load_sem, weight_sem, pair_send, pair_recv, outer_send, inner_send, mean_recv, diff_send, diff_recv,
+    part_send, part_recv, msg_send, msg_recv, tok_send, tok_recv, sum_send, sum_recv,
 ):
     seq = lax.axis_index("seq")
     tp = lax.axis_index("tp")
@@ -97,14 +97,23 @@
     loads[3].wait()
     pl.semaphore_wait(barrier, S - 1 + T - 1)
 
-    send_start = pl.multiple_of((1 - upper) * half, 8)
-    keep_start = pl.multiple_of(upper * half, 8)
-    grad_copy = remote(
-        grad.at[pl.ds(send_start, half)], partner_grad, pair_send.at[0], pair_recv.at[0],
-        (partner, tp),
+    keep = pl.ds(pl.multiple_of(upper * half, 8), half)
+    give = pl.ds(pl.multiple_of((1 - upper) * half, 8), half)
+
+    def grad_copy(h):
+        r = pl.ds(h * half, half)
+        return remote(
+            grad.at[r], partner_grad.at[r], pair_send.at[h], pair_recv.at[h], (partner, tp)
+        )
+
+    resid_copy = remote(
+        resid.at[give], partner_resid, pair_send.at[2], pair_recv.at[2], (partner, tp)
     )
-    resid_copy = remote(resid, partner_resid, pair_send.at[1], pair_recv.at[1], (partner, tp))
-    grad_copy.start()
+    score_copy = remote(
+        score_out, scored.at[upper], pair_send.at[3], pair_recv.at[3], (partner, tp)
+    )
+    grad_copy(0).start()
+    grad_copy(1).start()
 
     def diff_copy(block, c, step):
         place = diff.at[block, piece_rows(c)]
@@ -129,27 +138,43 @@
         @pl.when(tp - s >= 0)
         def _():
             diff_copy(tp - s, c, 1).wait_recv()
-            forward(tp - s, c, 1)
+            if s + 1 <= T - 2:
+                forward(tp - s, c, 1)
 
         @pl.when(tp + s < T)
         def _():
             diff_copy(tp + s, c, -1).wait_recv()
-            forward(tp + s, c, -1)
+            if s + 1 <= T - 2:
+                forward(tp + s, c, -1)
 
     each(C, lambda c: weight_load(c).start())
 
-    grad_copy.wait()
-    slot = lax.rem(seq, pairs) * 2 + upper
-    kept = grad[pl.ds(keep_start, half), :].astype(F32)
-    means[slot] = ((kept + partner_grad[...].astype(F32)) * 0.5).astype(BF16)
-
-    def mean_copy(i):
-        return remote(
-            means.at[slot], means.at[slot], mean_send.at[i], mean_recv.at[slot],
-            (lax.rem(seq + i, S), tp),
-        )
-
-    each(S - 1, lambda i: mean_copy(i + 1).start())
+    outer = pairs // 2
+    mine = lax.rem(seq, pairs)
+    chip = mine // 2
+    core = lax.rem(mine, 2)
+
+    def mean_copy(block, h, send, target):
+        place = means.at[block, pl.ds(h * half, half)]
+        return remote(place, place, send, mean_recv.at[block, h], (upper * pairs + target, tp))
+
+    def outer_copy(i, h):
+        return mean_copy(mine, h, outer_send.at[i, h], lax.rem(chip + i, outer) * 2 + core)
+
+    def inner_copy(i, h):
+        block = lax.rem(chip + i, outer) * 2 + core
+        return mean_copy(block, h, inner_send.at[i, h], chip * 2 + 1 - core)
+
+    def await_mean(block, h):
+        mean_copy(block, h, inner_send.at[0, h], chip * 2 + 1 - core).wait_recv()
+
+    for h in range(2):
+        grad_copy(h).wait()
+        r = pl.ds(h * half, half)
+        both = grad[r, :].astype(F32) + partner_grad[r, :].astype(F32)
+        means[mine, r, :] = (both * 0.5).astype(BF16)
+        each(outer - 1, lambda i: outer_copy(i + 1, h).start())
+        inner_copy(0, h).start()
     resid_copy.start()
 
     loads[4].wait()
@@ -178,28 +203,51 @@
     acc[...] = jnp.zeros_like(acc)
     token[...] = jnp.zeros_like(token)
 
-    each(C, lambda c: relay(1, c))
-
-    def await_mean(i):
-        source = lax.rem(seq + i + 1, S)
-        place = means.at[lax.rem(source, pairs) * 2 + source // pairs]
-        sem = mean_recv.at[lax.rem(source, pairs) * 2 + source // pairs]
-        remote(place, place, mean_send.at[0], sem, (source, tp)).wait_recv()
-
-    each(S - 1, await_mean)
-
-    def multiply(c):
+    each(C // 2, lambda c: relay(1, c))
+    for h in range(2):
+
+        def pass_on(i):
+            await_mean(lax.rem(chip + i + 1, outer) * 2 + core, h)
+            inner_copy(i + 1, h).start()
+
+        each(outer - 1, pass_on)
+    each(C - C // 2, lambda c: relay(1, c + C // 2))
+    for h in range(2):
+        each(outer, lambda i: await_mean(lax.rem(chip + i, outer) * 2 + 1 - core, h))
+
+    blocks = T // 2
+    at_end = (tp == 0) | (tp == T - 1)
+    far = jnp.where(tp == 0, T - 1, 0)
+    inward = jnp.where(tp == 0, 1, -1)
+
+    def partial_copy(c):
+        r = piece_rows(c)
+        return remote(
+            partial.at[r], partial_in.at[r], part_send.at[c], part_recv.at[c], (seq, tp + inward)
+        )
+
+    def multiply(side, c):
+        r = piece_rows(c)
+        right = means[pl.ds(side * outer, outer)]
+        right = right.reshape(outer * rows, right.shape[-1])
+        result = lax.dot_general(weight[r, :], right, NT, preferred_element_type=F32)
+        for k in range(blocks):
+            unit[side * blocks + k, r, :] = result[:, k * local_len : (k + 1) * local_len]
+
+    far_side = 1 - tp // blocks
+
+    def multiply_far(c):
         weight_load(c).wait()
-        r = piece_rows(c)
-        left = weight[r, :]
-        block_slots = 2 * pairs // T
-        for b in range(T):
-            right = means[b * block_slots : (b + 1) * block_slots]
-            right = right.reshape(local_len, right.shape[-1])
-            unit[b, r, :] = lax.dot_general(left, right, NT, preferred_element_type=F32)
-        relay(2, c)
-
-    each(C, multiply)
+        multiply(far_side, c)
+
+        @pl.when(at_end)
+        def _():
+            r = piece_rows(c)
+            partial[r, :] = unit[far, r, :].astype(BF16)
+            partial_copy(c).start()
+
+    each(C, multiply_far)
+    each(C, lambda c: multiply(1 - far_side, c))
 
     def product(block, c):
         r = piece_rows(c)
@@ -228,25 +276,46 @@
     resid_copy.wait()
     sign = (1 - 2 * upper).astype(F32)
 
-    def resid_rows(k):
-        r = pl.ds(pl.multiple_of(k * L, 8), L)
-        difference = resid[r, :].astype(F32) - partner_resid[r, :].astype(F32)
-        terms = sign * difference * grad[r, :].astype(F32)
+    difference = sign * (resid[keep, :].astype(F32) - partner_resid[...].astype(F32))
+
+    def score(gradient):
+        terms = difference * gradient.astype(F32)
         folded = terms[:, 0:128]
         for j in range(1, terms.shape[1] // 128):
             folded = folded + terms[:, j * 128 : (j + 1) * 128]
-        message[pl.ds(G + k, 1), :] = jnp.sum(folded.T, axis=0, keepdims=True)
-
-    each(R, resid_rows)
-    for s in range(min(3, T)):
-        each(C, lambda c: products(s, c))
-    for s in range(3, T):
+        return jnp.sum(folded.T, axis=0, keepdims=True)
+
+    score_out[...] = score(partner_grad[keep, :])
+    score_copy.start()
+    scored[upper] = score(grad[keep, :])
+    each(C, lambda c: products(0, c))
+    each(C, lambda c: products(1, c))
+    helped = ((tp == 1) | (tp == T - 2)) & (T > 2)
+    helped_block = jnp.where(tp == 1, T - 1, 0)
+
+    def help_in(c):
+        @pl.when(helped)
+        def _():
+            r = piece_rows(c)
+            remote(
+                partial.at[r], partial_in.at[r], part_send.at[c], part_recv.at[c],
+                (seq, jnp.where(tp == 1, 0, T - 1)),
+            ).wait_recv()
+            unit[helped_block, r, :] += partial_in[r, :].astype(F32)
+
+    for s in range(2, T - 1):
 
         def last(c):
             relay(s, c)
+            if s == T - 2:
+                help_in(c)
             products(s, c)
 
         each(C, last)
+    score_copy.wait()
+    message[G:, :] = jnp.zeros((2, L), F32)
+    for k in range(2):
+        message[G + k : G + k + 1, 0:half] = scored[k]
 
     def fold(g):
         block = acc[pl.ds(pl.multiple_of(g * L, 8), L), :]
@@ -299,7 +368,7 @@
     each(T - 1, await_message)
     total = jnp.sum(message_in[...], axis=0)
     neuron_out[...] = total[:G] * scales[2]
-    resid_out[...] = total[G:] * scales[0]
+    resid_out[...] = total[G:, 0:half] * scales[0]
 
     def await_sum(i):
         source = lax.rem(seq + i + 1, S)
@@ -310,7 +379,9 @@
     each(S - 1, await_sum)
     token_out[...] = jnp.sum(total_in[...], axis=0) * scales[1]
 
-    each(S - 1, lambda i: mean_copy(i + 1).wait_send())
+    for h in range(2):
+        each(outer - 1, lambda i: outer_copy(i + 1, h).wait_send())
+        each(outer, lambda i: inner_copy(i, h).wait_send())
     each(T - 1, lambda i: token_copy(i + 1).wait_send())
     each(T - 1, lambda i: message_copy(i + 1).wait_send())
     each(S - 1, lambda i: sum_copy(i + 1).wait_send())
@@ -321,11 +392,15 @@
             def _():
                 diff_copy(block, c, step).wait_send()
 
-        for s in range(T):
+        for s in range(T - 2):
             sent(tp - s, 1)
             sent(tp + s, -1)
 
     each(C, drain)
+
+    @pl.when(at_end)
+    def _():
+        each(C, lambda c: partial_copy(c).wait_send())
 
 
 def shards(grad_out, resid_in, down_weight, hidden_clean, hidden_corrupt, patched):
@@ -336,7 +411,6 @@
     C = max(c for c in range(1, 9) if units % (16 * c) == 0)
     L = math.gcd(units, 128)
     G = units // L
-    R = rows // L
     lanes = math.gcd(patched.shape[0], 1024)
     half = rows // 2
     scales = (
@@ -346,9 +420,9 @@
     )
     dma = lambda *shape: pltpu.SemaphoreType.DMA(shape)
     resid, token, neuron = pl.pallas_call(
-        functools.partial(kernel, S, T, C, G, L, R, scales),
+        functools.partial(kernel, S, T, C, G, L, scales),
         out_shape=(
-            jax.ShapeDtypeStruct((R, L), F32),
+            jax.ShapeDtypeStruct((2, half), F32),
             jax.ShapeDtypeStruct((1, local_len), F32),
             jax.ShapeDtypeStruct((G, L), F32),
         ),
@@ -361,21 +435,26 @@
             pltpu.VMEM((units, local_len), BF16),
             pltpu.VMEM((units, local_len), BF16),
             pltpu.VMEM((patched.shape[0] // lanes, lanes), jnp.int32),
+            pltpu.VMEM((rows, width), BF16),
             pltpu.VMEM((half, width), BF16),
-            pltpu.VMEM((rows, width), BF16),
-            pltpu.VMEM((S, half, width), BF16),
+            pltpu.VMEM((S // 2, rows, width), BF16),
             pltpu.VMEM((T, units, local_len), BF16),
             pltpu.VMEM((T, units, local_len), F32),
+            pltpu.VMEM((units, local_len), BF16),
+            pltpu.VMEM((units, local_len), BF16),
             pltpu.VMEM((units, 128), F32),
             pltpu.VMEM((units, 128), F32),
             pltpu.VMEM((T, 1, local_len), F32),
             pltpu.VMEM((T, 1, local_len), F32),
             pltpu.VMEM((1, local_len), F32),
             pltpu.VMEM((S, 1, local_len), F32),
-            pltpu.VMEM((G + R, L), F32),
-            pltpu.VMEM((T, G + R, L), F32),
+            pltpu.VMEM((G + 2, L), F32),
+            pltpu.VMEM((T, G + 2, L), F32),
             pltpu.VMEM((G, L), F32),
-            dma(5), dma(C), dma(2), dma(2), dma(S), dma(S), dma(2, T, C), dma(T, C),
+            pltpu.VMEM((2, 1, half), F32),
+            pltpu.VMEM((1, half), F32),
+            dma(5), dma(C), dma(4), dma(4), dma(S // 4, 2), dma(S // 4, 2), dma(S // 2, 2),
+            dma(2, T, C), dma(T, C), dma(C), dma(C),
             dma(T), dma(T), dma(T), dma(T), dma(S), dma(S),
         ],
         compiler_params=pltpu.CompilerParams(

time: 81.8 us -> 64.5 us (0.79)
  Pallas kernels: 75.8 us -> 58.4 us
    pallas_call x1, Pallas kernels: 75.8 us -> 58.4 us  [shards(): pl.pallas_call(functools.partial(kernel, S, T, C, G, L, scales), out_shap...]
    reshape x0 -> x1, local copies, waits for them, and re-layouts: none -> 1.25 us  [shards(): resid.reshape(rows)]
    unnamed x3 -> x2, local copies, waits for them, and re-layouts: 3.62 us -> 2.51 us
where the time goes in v1:
time: 64.5 us; the launch traced here: 64.3 us
  Pallas kernels  58.4 us (91%)
  local copies, waits for them, and re-layouts  5.22 us (8%)
    pallas_call x1, Pallas kernels, shards(): pl.pallas_call(functools.partial(kernel, S, T, C, G, L, scales), out_shap...  58.4 us
    unnamed x2, local copies, waits for them, and re-layouts  2.51 us
    reshape x1, local copies, waits for them, and re-layouts, shards(): patched.reshape(-1, lanes)  1.45 us

profile of v1, /device:TPU:0, one launch (start us, length us, event | category | flops | bytes accessed | tf_op | source)
XLA Modules:
  0.0 64.3 jit_solution(604392190004674417)
XLA Ops:
  0.6 1.4 %reshape.18.patched_hbm = s32[14,1024]{1,0:T(8,128)} reshape(s32[14336]{0:T(1024)} %param.11) | data formatting | bytes 114688 | tf_op jit(solution)/shard_map/reshape | solution.py:465
  2.1 58.4 %shard_map.85 = (f32[2,64]{1,0:T(2,128)}, f32[1,128]{1,0:T(1,128)}, f32[28,128]{1,0:T(8,128)}) custom-call(bf16[128,2048]{1,0:T(8,128)(2,1)} %grad_hbm.1, bf16[128,2048]{1,0:T(8,128)(2,1)} %resid_hbm.1, bf16[3584,2048]{1,0:T(8,128)(2,1)} %weight_hbm.1, bf16[3584,128]{1,0:T(8,128)(2,1)} %clean_hbm.1, bf16[3584,128]{1,0:T(8,128)(2,1)} %corrupt_hbm.1, ...), custom_call_target="tpu_custom_call" | custom-call | tf_op jit(solution)/shard_map/pallas_call | solution.py:422
  60.5 1.3 %reshape.19 = f32[128]{0:T(128)} reshape(f32[2,64]{1,0:T(2,128)} %get-tuple-element.6) | data formatting | bytes 1024 | tf_op jit(solution)/shard_map/reshape | solution.py:467
  61.8 1.2 %copy.11 = f32[128]{0:T(128)} copy(f32[128]{0:T(128)} %bitcast.3) | data formatting | bytes 1024
  62.9 1.3 %copy.12 = f32[3584]{0:T(1024)} copy(f32[3584]{0:T(1024)} %bitcast.2) | data formatting | bytes 28672

commit v2 on v1

--- a/solution.py
+++ b/solution.py
@@ -24,7 +24,7 @@
 def kernel(
     S, T, C, G, L, scales,
     grad_hbm, resid_hbm, weight_hbm, clean_hbm, corrupt_hbm, patched_hbm,
-    resid_out, token_out, neuron_out,
+    scores,
     grad, resid, weight, clean, corrupt, patched,
     partner_grad, partner_resid, means, diff, unit, partial, partial_in, mask, acc, token, token_in, token_sum,
     total_in, message, message_in, counts, scored, score_out,
@@ -42,6 +42,8 @@
     piece = units // C
     local_len = diff.shape[2]
 
+    lanes = patched.shape[2]
+
     def local(source, target, index):
         return pltpu.make_async_copy(source, target, load_sem.at[index])
 
@@ -50,10 +52,14 @@
         local(corrupt_hbm, corrupt, 1),
         local(grad_hbm, grad, 2),
         local(resid_hbm, resid, 3),
-        local(patched_hbm, patched, 4),
     ]
-    for load in loads:
-        load.start()
+    for index in (2, 0, 1, 3):
+        loads[index].start()
+
+    def ids_load(k):
+        return local(patched_hbm.at[pl.ds(pl.multiple_of(k * lanes, lanes), lanes)], patched.at[k, 0], 4 + k)
+
+    each(patched.shape[0], lambda k: ids_load(k).start())
 
     def piece_rows(c):
         return pl.ds(pl.multiple_of(c * piece, 16), piece)
@@ -85,18 +91,8 @@
 
     each(S - 1, greet_seq)
     each(T - 1, greet_tp)
-    loads[0].wait()
-    loads[1].wait()
-
-    def subtract(c):
-        r = piece_rows(c)
-        diff[tp, r, :] = (clean[r, :].astype(F32) - corrupt[r, :].astype(F32)).astype(BF16)
-
-    each(C, subtract)
     loads[2].wait()
-    loads[3].wait()
     pl.semaphore_wait(barrier, S - 1 + T - 1)
-
     keep = pl.ds(pl.multiple_of(upper * half, 8), half)
     give = pl.ds(pl.multiple_of((1 - upper) * half, 8), half)
 
@@ -132,7 +128,15 @@
         forward(tp, c, 1)
         forward(tp, c, -1)
 
-    each(C, own)
+    loads[0].wait()
+    loads[1].wait()
+
+    def subtract(c):
+        r = piece_rows(c)
+        diff[tp, r, :] = (clean[r, :].astype(F32) - corrupt[r, :].astype(F32)).astype(BF16)
+        own(c)
+
+    each(C, subtract)
 
     def relay(s, c):
         @pl.when(tp - s >= 0)
@@ -175,16 +179,16 @@
         means[mine, r, :] = (both * 0.5).astype(BF16)
         each(outer - 1, lambda i: outer_copy(i + 1, h).start())
         inner_copy(0, h).start()
+    loads[3].wait()
     resid_copy.start()
 
-    loads[4].wait()
+    each(patched.shape[0], lambda k: ids_load(k).wait())
     counts[...] = jnp.zeros_like(counts)
-    width = patched.shape[1]
-    group_ids = lax.broadcasted_iota(jnp.int32, (G, width), 0)
-    lane_ids = lax.broadcasted_iota(jnp.int32, (L, width), 0)
+    group_ids = lax.broadcasted_iota(jnp.int32, (G, lanes), 0)
+    lane_ids = lax.broadcasted_iota(jnp.int32, (L, lanes), 0)
 
     def count(k):
-        ids = patched[pl.ds(k, 1), :] - seq * units + S * units
+        ids = patched[k] - seq * units + S * units
         high = ids // L - (S * units) // L
         low = lax.rem(ids, L)
         counts[...] += lax.dot_general(
@@ -303,6 +307,15 @@
             ).wait_recv()
             unit[helped_block, r, :] += partial_in[r, :].astype(F32)
 
+    def fold(g):
+        block = acc[pl.ds(pl.multiple_of(g * L, 8), L), :]
+        message[pl.ds(g, 1), :] = jnp.sum(block.T, axis=0, keepdims=True)
+
+    score_copy.wait()
+    message[G:, :] = jnp.zeros((2, L), F32)
+    for k in range(2):
+        message[G + k : G + k + 1, 0:half] = scored[k]
+
     for s in range(2, T - 1):
 
         def last(c):
@@ -310,17 +323,10 @@
             if s == T - 2:
                 help_in(c)
             products(s, c)
+            if s == T - 2:
+                each(G // C, lambda g: fold(c * (G // C) + g))
 
         each(C, last)
-    score_copy.wait()
-    message[G:, :] = jnp.zeros((2, L), F32)
-    for k in range(2):
-        message[G + k : G + k + 1, 0:half] = scored[k]
-
-    def fold(g):
-        block = acc[pl.ds(pl.multiple_of(g * L, 8), L), :]
-        message[pl.ds(g, 1), :] = jnp.sum(block.T, axis=0, keepdims=True)
-
     def token_copy(i):
         target = lax.rem(tp + i, T)
         return remote(
@@ -328,7 +334,6 @@
         )
 
     each(T - 1, lambda i: token_copy(i + 1).start())
-    each(G, fold)
 
     def message_copy(i):
         return remote(
@@ -339,6 +344,25 @@
     each(T - 1, lambda i: message_copy(i + 1).start())
 
     token_in[tp] = token[tp]
+    for h in range(2):
+        each(outer - 1, lambda i: outer_copy(i + 1, h).wait_send())
+        each(outer, lambda i: inner_copy(i, h).wait_send())
+
+    def drain(c):
+        def sent(block, step):
+            @pl.when((tp + step >= 0) & (tp + step < T) & (block >= 0) & (block < T))
+            def _():
+                diff_copy(block, c, step).wait_send()
+
+        for s in range(T - 2):
+            sent(tp - s, 1)
+            sent(tp + s, -1)
+
+    each(C, drain)
+
+    @pl.when(at_end)
+    def _():
+        each(C, lambda c: partial_copy(c).wait_send())
 
     def await_token(i):
         source = lax.rem(tp + i + 1, T)
@@ -367,8 +391,8 @@
 
     each(T - 1, await_message)
     total = jnp.sum(message_in[...], axis=0)
-    neuron_out[...] = total[:G] * scales[2]
-    resid_out[...] = total[G:, 0:half] * scales[0]
+    scores[0:G, :] = total[:G] * scales[2]
+    scores[G : G + 2, :] = total[G:] * scales[0]
 
     def await_sum(i):
         source = lax.rem(seq + i + 1, S)
@@ -377,30 +401,22 @@
         ).wait_recv()
 
     each(S - 1, await_sum)
-    token_out[...] = jnp.sum(total_in[...], axis=0) * scales[1]
-
-    for h in range(2):
-        each(outer - 1, lambda i: outer_copy(i + 1, h).wait_send())
-        each(outer, lambda i: inner_copy(i, h).wait_send())
+    token_total = jnp.sum(total_in[...], axis=0) * scales[1]
+    for k in range(local_len // L):
+        scores[G + 2 + k : G + 3 + k, :] = token_total[:, k * L : (k + 1) * L]
+
     each(T - 1, lambda i: token_copy(i + 1).wait_send())
     each(T - 1, lambda i: message_copy(i + 1).wait_send())
     each(S - 1, lambda i: sum_copy(i + 1).wait_send())
 
-    def drain(c):
-        def sent(block, step):
-            @pl.when((tp + step >= 0) & (tp + step < T) & (block >= 0) & (block < T))
-            def _():
-                diff_copy(block, c, step).wait_send()
-
-        for s in range(T - 2):
-            sent(tp - s, 1)
-            sent(tp + s, -1)
-
-    each(C, drain)
-
-    @pl.when(at_end)
-    def _():
-        each(C, lambda c: partial_copy(c).wait_send())
+
+def write(G, K, L, half, scores, resid_out, token_out, neuron_out):
+    for k in range(2):
+        resid_out[k * half : (k + 1) * half] = scores[G + k, 0:half]
+    for k in range(K):
+        token_out[k * L : (k + 1) * L] = scores[G + 2 + k, :]
+    for g in range(G):
+        neuron_out[g * L : (g + 1) * L] = scores[g, :]
 
 
 def shards(grad_out, resid_in, down_weight, hidden_clean, hidden_corrupt, patched):
@@ -408,9 +424,9 @@
     T = lax.axis_size("tp")
     rows, width = grad_out.shape
     units, local_len = hidden_clean.shape
-    C = max(c for c in range(1, 9) if units % (16 * c) == 0)
     L = math.gcd(units, 128)
     G = units // L
+    C = max(c for c in range(1, 9) if G % c == 0)
     lanes = math.gcd(patched.shape[0], 1024)
     half = rows // 2
     scales = (
@@ -419,22 +435,19 @@
         1.0 / math.sqrt(local_len * T),
     )
     dma = lambda *shape: pltpu.SemaphoreType.DMA(shape)
-    resid, token, neuron = pl.pallas_call(
+    K = local_len // L
+    scores = pl.pallas_call(
         functools.partial(kernel, S, T, C, G, L, scales),
-        out_shape=(
-            jax.ShapeDtypeStruct((2, half), F32),
-            jax.ShapeDtypeStruct((1, local_len), F32),
-            jax.ShapeDtypeStruct((G, L), F32),
-        ),
+        out_shape=jax.ShapeDtypeStruct((G + 2 + K, L), F32),
         in_specs=[pl.BlockSpec(memory_space=pl.ANY)] * 6,
-        out_specs=[pl.BlockSpec(memory_space=pltpu.VMEM)] * 3,
+        out_specs=pl.BlockSpec(memory_space=pltpu.VMEM),
         scratch_shapes=[
             pltpu.VMEM((rows, width), BF16),
             pltpu.VMEM((rows, width), BF16),
             pltpu.VMEM((units, width), BF16),
             pltpu.VMEM((units, local_len), BF16),
             pltpu.VMEM((units, local_len), BF16),
-            pltpu.VMEM((patched.shape[0] // lanes, lanes), jnp.int32),
+            pltpu.VMEM((patched.shape[0] // lanes, 1, lanes), jnp.int32),
             pltpu.VMEM((rows, width), BF16),
             pltpu.VMEM((half, width), BF16),
             pltpu.VMEM((S // 2, rows, width), BF16),
@@ -453,7 +466,7 @@
             pltpu.VMEM((G, L), F32),
             pltpu.VMEM((2, 1, half), F32),
             pltpu.VMEM((1, half), F32),
-            dma(5), dma(C), dma(4), dma(4), dma(S // 4, 2), dma(S // 4, 2), dma(S // 2, 2),
+            dma(4 + patched.shape[0] // lanes), dma(C), dma(4), dma(4), dma(S // 4, 2), dma(S // 4, 2), dma(S // 2, 2),
             dma(2, T, C), dma(T, C), dma(C), dma(C),
             dma(T), dma(T), dma(T), dma(T), dma(S), dma(S),
         ],
@@ -462,9 +475,18 @@
         ),
     )(
         grad_out, resid_in, down_weight, hidden_clean, hidden_corrupt,
-        patched.reshape(-1, lanes),
+        patched,
     )
-    return (resid.reshape(rows), token.reshape(local_len), neuron.reshape(units))
+    return pl.pallas_call(
+        functools.partial(write, G, K, L, half),
+        out_shape=(
+            jax.ShapeDtypeStruct((rows,), F32),
+            jax.ShapeDtypeStruct((local_len,), F32),
+            jax.ShapeDtypeStruct((units,), F32),
+        ),
+        in_specs=[pl.BlockSpec(memory_space=pltpu.VMEM)],
+        out_specs=[pl.BlockSpec(memory_space=pltpu.VMEM)] * 3,
+    )(scores)
 
 
 def solution(mesh):

time: 64.5 us -> 61.5 us (0.953)
  local copies, waits for them, and re-layouts: 5.22 us -> 0 us
  Pallas kernels: 58.4 us -> 60.7 us
    reshape x2 -> x0, local copies, waits for them, and re-layouts: 2.7 us -> none  [the longest x1 1.45 us: shards(): patched.reshape(-1, lanes)]
    unnamed x2 -> x0, local copies, waits for them, and re-layouts: 2.51 us -> none
    pallas_call x0 -> x1, Pallas kernels: none -> 1.33 us  [shards(): pl.pallas_call(functools.partial(write, G, K, L, half), out_shape=(jax.Sh...]
    pallas_call x1, Pallas kernels: 58.4 us -> 59.3 us  [shards(): pl.pallas_call(functools.partial(kernel, S, T, C, G, L, scales), out_shap...]
where the time goes in v2:
time: 61.5 us; the launch traced here: 61.3 us
  Pallas kernels  60.7 us (99%)
  between operations  0.64 us (1%)
    pallas_call x1, Pallas kernels, shards(): pl.pallas_call(functools.partial(kernel, S, T, C, G, L, scales), out_shap...  59.3 us
    pallas_call x1, Pallas kernels, shards(): pl.pallas_call(functools.partial(write, G, K, L, half), out_shape=(jax.Sh...  1.33 us

profile of v2, /device:TPU:0, one launch (start us, length us, event | category | flops | bytes accessed | tf_op | source)
XLA Modules:
  0.0 61.3 jit_solution(2774944633767220167)
XLA Ops:
  0.6 59.3 %shard_map.85.scores = f32[31,128]{1,0:T(8,128)} custom-call(bf16[128,2048]{1,0:T(8,128)(2,1)} %grad_hbm.1, bf16[128,2048]{1,0:T(8,128)(2,1)} %resid_hbm.1, bf16[3584,2048]{1,0:T(8,128)(2,1)} %weight_hbm.1, bf16[3584,128]{1,0:T(8,128)(2,1)} %clean_hbm.1, bf16[3584,128]{1,0:T(8,128)(2,1)} %corrupt_hbm.1, s32[14336]{0:T(1024)} %patched_hbm.1), custom_call_target="tpu_custom_call" | custom-call | tf_op jit(solution)/shard_map/pallas_call | solution.py:439
  60.0 1.3 %shard_map.86 = (f32[128]{0:T(128)}, f32[128]{0:T(128)}, f32[3584]{0:T(1024)}) custom-call(f32[31,128]{1,0:T(8,128)} %shard_map.85.scores), custom_call_target="tpu_custom_call" | custom-call | tf_op jit(solution)/shard_map/pallas_call | solution.py:480

commit v3 on v2

--- a/solution.py
+++ b/solution.py
@@ -215,7 +215,6 @@
             inner_copy(i + 1, h).start()
 
         each(outer - 1, pass_on)
-    each(C - C // 2, lambda c: relay(1, c + C // 2))
     for h in range(2):
         each(outer, lambda i: await_mean(lax.rem(chip + i, outer) * 2 + 1 - core, h))
 
@@ -250,7 +249,13 @@
             partial[r, :] = unit[far, r, :].astype(BF16)
             partial_copy(c).start()
 
-    each(C, multiply_far)
+    each(C // 2, multiply_far)
+
+    def multiply_and_relay(c):
+        multiply_far(c + C // 2)
+        relay(1, c + C // 2)
+
+    each(C - C // 2, multiply_and_relay)
     each(C, lambda c: multiply(1 - far_side, c))
 
     def product(block, c):

time: 61.5 us -> 59.5 us (0.967)
  Pallas kernels: 60.7 us -> 58.6 us
    pallas_call x1, Pallas kernels: 59.3 us -> 57.3 us  [shards(): pl.pallas_call(functools.partial(kernel, S, T, C, G, L, scales), out_shap...]
where the time goes in v3:
time: 59.5 us; the launch traced here: 59.3 us
  Pallas kernels  58.6 us (98%)
  between operations  0.64 us (1%)
    pallas_call x1, Pallas kernels, shards(): pl.pallas_call(functools.partial(kernel, S, T, C, G, L, scales), out_shap...  57.3 us
    pallas_call x1, Pallas kernels, shards(): pl.pallas_call(functools.partial(write, G, K, L, half), out_shape=(jax.Sh...  1.33 us

profile of v3, /device:TPU:0, one launch (start us, length us, event | category | flops | bytes accessed | tf_op | source)
XLA Modules:
  0.0 59.3 jit_solution(8740758216104420681)
XLA Ops:
  0.6 57.3 %shard_map.85.scores = f32[31,128]{1,0:T(8,128)} custom-call(bf16[128,2048]{1,0:T(8,128)(2,1)} %grad_hbm.1, bf16[128,2048]{1,0:T(8,128)(2,1)} %resid_hbm.1, bf16[3584,2048]{1,0:T(8,128)(2,1)} %weight_hbm.1, bf16[3584,128]{1,0:T(8,128)(2,1)} %clean_hbm.1, bf16[3584,128]{1,0:T(8,128)(2,1)} %corrupt_hbm.1, s32[14336]{0:T(1024)} %patched_hbm.1), custom_call_target="tpu_custom_call" | custom-call | tf_op jit(solution)/shard_map/pallas_call | solution.py:444
  58.0 1.3 %shard_map.86 = (f32[128]{0:T(128)}, f32[128]{0:T(128)}, f32[3584]{0:T(1024)}) custom-call(f32[31,128]{1,0:T(8,128)} %shard_map.85.scores), custom_call_target="tpu_custom_call" | custom-call | tf_op jit(solution)/shard_map/pallas_call | solution.py:485
